TPU v7x, 256 devices: a whole 4x4x8 slice. The times are simulated.
256 devices in a mesh: ctx: 32 (over z, x_lo, core), head: 8 (over x_hi, y).
Axes of the slice: x: 4 (x_hi: 2, x_lo: 2; x = x_hi * 2 + x_lo), y: 4, z: 8, core: 2. Of those that a mesh axis runs over, the one named last changes fastest.
Arguments:
- queries: bfloat16 [8192, 24, 128], P('ctx', 'head'), may hold values from -4.5 to 4.5, as said below
- key_vectors: bfloat16 [8192, 24, 128], P('ctx', 'head'), may hold values from -4.5 to 4.5, as said below
- value_vectors: bfloat16 [8192, 24, 128], P('ctx', 'head'), may hold values from -6 to 6
- attn_output: bfloat16 [8192, 24, 128], P('ctx', 'head'), may hold values from -6 to 6
- output_grad: bfloat16 [8192, 5120], P('ctx', 'head'), may hold values from -6 to 6
- w_out: bfloat16 [3072, 5120], P('head'), may hold values from -0.078125 to 0.078125
- log_total: float32 [8192, 24], P('ctx', 'head'), as said below
Outputs:
- query_grad: bfloat16 [8192, 24, 128], P('ctx', 'head')
- key_grad: bfloat16 [8192, 24, 128], P('ctx', 'head')
- value_grad: bfloat16 [8192, 24, 128], P('ctx', 'head')
Inputs may be any that keep to these rules, and one draw needn't show every extreme that they name: `queries`: independent entries of order one. `key_vectors`: entries of order one. `log_total`: for each position and head, the log of the sum of exp(scores) over the positions it sees, from the given queries and keys.
All inputs are finite; a program needn't handle non-finite values.
Results may differ from a plain program's by a relative error of at most 0.0058.
Values may be sent and summed in bfloat16 or wider, within the bound.
A program may use at most 128 MiB of HBM per device.

v0:
```python
import jax
import jax.numpy as jnp
from jax import lax
from jax.sharding import PartitionSpec as P


def block_terms(
    query_block,
    grad_block,
    total_block,
    delta_block,
    key_block,
    value_block,
    query_pos,
    key_pos,
    factor,
):
    raw_scores = (
        jnp.einsum("qhd,khd->hqk", query_block, key_block, preferred_element_type=jnp.float32)
        * factor
    )
    visible = key_pos[None, None, :] <= query_pos[None, :, None]
    scores = jnp.where(visible, raw_scores, -jnp.inf)
    prob_full = jnp.exp(scores - total_block[:, :, None])
    prob_grad = jnp.einsum(
        "qhd,khd->hqk", grad_block, value_block, preferred_element_type=jnp.float32
    )
    score_grad = (prob_full * (prob_grad - delta_block[:, :, None])).astype(jnp.bfloat16)
    return (prob_full.astype(jnp.bfloat16), score_grad)


def query_pass(query_group, gathered_keys, gathered_values, span_rows, factor):
    query_rows, grad_rows, total_rows, delta_rows, query_pos = query_group
    highest = jnp.max(query_pos)

    def query_advance(step_index, running):
        offset = step_index * span_rows

        def query_update(query_grad):
            key_block = lax.dynamic_slice_in_dim(gathered_keys, offset, span_rows, 0)
            value_block = lax.dynamic_slice_in_dim(gathered_values, offset, span_rows, 0)
            key_pos = offset + jnp.arange(span_rows, dtype=jnp.int32)
            prob_low, score_grad = block_terms(
                query_rows,
                grad_rows,
                total_rows,
                delta_rows,
                key_block,
                value_block,
                query_pos,
                key_pos,
                factor,
            )
            return (
                query_grad
                + jnp.einsum(
                    "hqk,khd->qhd", score_grad, key_block, preferred_element_type=jnp.float32
                )
                * factor
            )

        return lax.cond(offset <= highest, query_update, lambda carried: carried, running)

    initial = jnp.zeros(query_rows.shape, jnp.float32)
    return lax.fori_loop(0, gathered_keys.shape[0] // span_rows, query_advance, initial)


def key_pass(
    own_keys, own_values, key_pos, all_queries, all_grads, all_totals, all_deltas, span_rows, factor
):
    lowest = jnp.min(key_pos)

    def key_advance(step_index, running):
        offset = step_index * span_rows

        def key_update(carried):
            key_grad, value_grad = carried
            query_block = lax.dynamic_slice_in_dim(all_queries, offset, span_rows, 0)
            grad_block = lax.dynamic_slice_in_dim(all_grads, offset, span_rows, 0)
            total_block = lax.dynamic_slice_in_dim(all_totals, offset, span_rows, 1)
            delta_block = lax.dynamic_slice_in_dim(all_deltas, offset, span_rows, 1)
            query_pos = offset + jnp.arange(span_rows, dtype=jnp.int32)
            prob_low, score_grad = block_terms(
                query_block,
                grad_block,
                total_block,
                delta_block,
                own_keys,
                own_values,
                query_pos,
                key_pos,
                factor,
            )
            key_grad = (
                key_grad
                + jnp.einsum(
                    "hqk,qhd->khd", score_grad, query_block, preferred_element_type=jnp.float32
                )
                * factor
            )
            value_grad = value_grad + jnp.einsum(
                "hqk,qhd->khd", prob_low, grad_block, preferred_element_type=jnp.float32
            )
            return (key_grad, value_grad)

        return lax.cond(
            offset + span_rows - 1 >= lowest, key_update, lambda carried: carried, running
        )

    initial = (jnp.zeros(own_keys.shape, jnp.float32), jnp.zeros(own_values.shape, jnp.float32))
    return lax.fori_loop(0, all_queries.shape[0] // span_rows, key_advance, initial)


def body(queries, key_vectors, value_vectors, attn_output, output_grad, w_out, log_total):
    local_rows, head_count, head_width = queries.shape
    factor = head_width ** (-0.5)
    ctx_count = lax.axis_size("ctx")
    ctx_index = lax.axis_index("ctx")
    total_len = local_rows * ctx_count
    span_rows = min(512, total_len)
    grad_flat = jnp.einsum(
        "tc,rc->tr",
        lax.all_gather(output_grad, "head", axis=1, tiled=True),
        w_out,
        preferred_element_type=jnp.float32,
    )
    attn_grad = grad_flat.astype(jnp.bfloat16).reshape(local_rows, head_count, head_width)
    row_delta = jnp.einsum(
        "qhd,qhd->hq", attn_grad, attn_output, preferred_element_type=jnp.float32
    )
    own_total = jnp.transpose(log_total, (1, 0))
    own_pos = ctx_index * local_rows + jnp.arange(local_rows, dtype=jnp.int32)
    groups = [(queries, attn_grad, own_total, row_delta, own_pos)]
    gathered_keys, gathered_values = (
        lax.all_gather(key_vectors, "ctx", axis=0, tiled=True),
        lax.all_gather(value_vectors, "ctx", axis=0, tiled=True),
    )
    partial_grads = [
        query_pass(query_group, gathered_keys, gathered_values, span_rows, factor)
        for query_group in groups
    ]
    all_queries, all_grads = (
        lax.all_gather(queries, "ctx", axis=0, tiled=True),
        lax.all_gather(attn_grad, "ctx", axis=0, tiled=True),
    )
    all_totals, all_deltas = (
        lax.all_gather(own_total, "ctx", axis=1, tiled=True),
        lax.all_gather(row_delta, "ctx", axis=1, tiled=True),
    )
    key_part, value_part = key_pass(
        key_vectors,
        value_vectors,
        own_pos,
        all_queries,
        all_grads,
        all_totals,
        all_deltas,
        span_rows,
        factor,
    )
    results = [piece.astype(jnp.bfloat16) for piece in partial_grads]
    query_grad = results[0]
    return (query_grad, key_part.astype(jnp.bfloat16), value_part.astype(jnp.bfloat16))


def solution(mesh):
    in_specs = (
        P("ctx", "head", None),
        P("ctx", "head", None),
        P("ctx", "head", None),
        P("ctx", "head", None),
        P("ctx", "head"),
        P("head", None),
        P("ctx", "head"),
    )
    out_specs = (P("ctx", "head", None), P("ctx", "head", None), P("ctx", "head", None))
    return jax.shard_map(body, mesh=mesh, in_specs=in_specs, out_specs=out_specs, check_vma=False)
```

profile of v0, /device:TPU:1, one launch (start us, length us, event | category | flops | bytes accessed | tf_op | source)
XLA Modules:
  0.0 466.0 jit_solution(10017530869229409577)
XLA Ops:
  9.4 67.1 %all-gather.10.cloned.1.call-done = bf16[256,5120]{1,0:T(8,128)(2,1)} async-done(((bf16[256,640]{1,0:T(8,128)(2,1)}), bf16[256,5120]{1,0:T(8,128)(2,1)}) %all-gather.10.cloned.1.call-update) | async-done | bytes 2621456 | tf_op jit(solution)/shard_map/all_gather | solution.py:123
  76.6 4.4 convolution_convert_fusion
  83.8 35.6 %all_gather.25 = f32[3,8192]{1,0:T(4,128)S(1)} all-gather(f32[3,256]{1,0:T(4,128)S(1)} %bitcast.56), channel_id=1, replica_groups=mesh['ctx'=32,'head'=8] {'ctx'}, dimensions={1}, use_global_device_ids=true | all-gather | bytes 101376 | tf_op jit(solution)/shard_map/all_gather | solution.py:147
  121.8 31.2 %all_gather.27 = f32[3,8192]{1,0:T(4,128)S(1)} all-gather(f32[3,256]{1,0:T(4,128)S(1)} %multiply_reduce_fusion), channel_id=1, replica_groups=mesh['ctx'=32,'head'=8] {'ctx'}, dimensions={1}, use_global_device_ids=true | all-gather | bytes 101376 | tf_op jit(solution)/shard_map/all_gather | solution.py:148
  153.0 64.4 %all-gather.8.cloned.1.call-done = bf16[8192,3,128]{2,0,1:T(8,128)(2,1)} async-done(((bf16[256,3,128]{2,0,1:T(8,128)(2,1)}), bf16[8192,3,128]{2,0,1:T(8,128)(2,1)}) %all-gather.8.cloned.1.call-update) | async-done | bytes 6291472 | tf_op jit(solution)/shard_map/all_gather | solution.py:136
  217.4 14.6 %while.37 = (s32[]{:T(128)}, f32[256,3,128]{0,2,1:T(8,128)S(1)}, s32[]{:T(128)}, bf16[8192,3,128]{2,0,1:T(8,128)(2,1)}, bf16[256,3,128]{2,0,1:T(8,128)(2,1)S(1)}...) while((s32[]{:T(128)}, f32[256,3,128]{0,2,1:T(8,128)S(1)}, ...), condition=%wide.region_4.5_spmd.clone, body=%wide.region_1.4_spmd.clone.sunk | while | flops 304677632 | bytes 5782805 | solution.py:65
  218.1 3.5 conditional.6
  219.7 2.0 fusion.10
  232.9 66.2 %all-gather.14.cloned.1.call-done = bf16[8192,3,128]{0,2,1:T(8,128)(2,1)} async-done(((bf16[256,3,128]{0,2,1:T(8,128)(2,1)}), bf16[8192,3,128]{0,2,1:T(8,128)(2,1)}) %all-gather.14.cloned.1.call-update) | async-done | bytes 6291472 | tf_op jit(solution)/shard_map/all_gather | solution.py:144
  299.1 8.6 %copy.36 = bf16[8192,3,128]{2,0,1:T(8,128)(2,1)} copy(bf16[8192,3,128]{0,2,1:T(8,128)(2,1)} %all-gather.14.cloned.1.call-done) | data formatting | bytes 12582912
  307.7 60.7 %all-gather.12.cloned.1.call-done = bf16[8192,3,128]{2,0,1:T(8,128)(2,1)} async-done(((bf16[256,3,128]{2,0,1:T(8,128)(2,1)}), bf16[8192,3,128]{2,0,1:T(8,128)(2,1)}) %all-gather.12.cloned.1.call-update) | async-done | bytes 6291472 | tf_op jit(solution)/shard_map/all_gather | solution.py:143
  368.5 89.4 %while.38 = (s32[]{:T(128)}, f32[256,3,128]{0,2,1:T(8,128)S(1)}, f32[256,3,128]{0,2,1:T(8,128)S(1)}, s32[]{:T(128)}, bf16[8192,3,128]{2,0,1:T(8,128)(2,1)}, /*in...) while((s32[]{:T(128)}, f32[256,3,128]{0,2,1:T(8,128)S(1)}, ...), condition=%wide.region_9.10_spmd.clone, body=%wide.region_6.9_spmd.clone.sunk | while | flops 405832448 | bytes 8566113 | solution.py:111
  369.1 4.9 %conditional.7 = ((f32[256,3,128]{0,2,1:T(8,128)S(1)}, f32[256,3,128]{0,2,1:T(8,128)S(1)})) conditional(s32[]{:T(128)} %convert_element_type.71, (f32[256,3,128]{0,2,1:T(8,128)S(1)}, f32[256,3,128]{0,2,1:T(8,128)S(1)}) %tuple.108, (s32[]{:T(128)}, bf16[8192,3,128]{2,0,1:T(8,128)(2,1)}, s32[]{:T(128)}, bf16[256,3,128]{2,0,1:T(8,128)(2,1)S(1)}, ...), branch_computations={%region_7.7_spmd, %region_8.8_spmd} | conditional | flops 405832448 | bytes 8564814 | solution.py:106
  372.2 1.8 fusion.30
  374.7 4.9 %conditional.7 = ((f32[256,3,128]{0,2,1:T(8,128)S(1)}, f32[256,3,128]{0,2,1:T(8,128)S(1)})) conditional(s32[]{:T(128)} %convert_element_type.71, (f32[256,3,128]{0,2,1:T(8,128)S(1)}, f32[256,3,128]{0,2,1:T(8,128)S(1)}) %tuple.108, (s32[]{:T(128)}, bf16[8192,3,128]{2,0,1:T(8,128)(2,1)}, s32[]{:T(128)}, bf16[256,3,128]{2,0,1:T(8,128)(2,1)S(1)}, ...), branch_computations={%region_7.7_spmd, %region_8.8_spmd} | conditional | flops 405832448 | bytes 8564814 | solution.py:106
  380.3 4.9 %conditional.7 = ((f32[256,3,128]{0,2,1:T(8,128)S(1)}, f32[256,3,128]{0,2,1:T(8,128)S(1)})) conditional(s32[]{:T(128)} %convert_element_type.71, (f32[256,3,128]{0,2,1:T(8,128)S(1)}, f32[256,3,128]{0,2,1:T(8,128)S(1)}) %tuple.108, (s32[]{:T(128)}, bf16[8192,3,128]{2,0,1:T(8,128)(2,1)}, s32[]{:T(128)}, bf16[256,3,128]{2,0,1:T(8,128)(2,1)S(1)}, ...), branch_computations={%region_7.7_spmd, %region_8.8_spmd} | conditional | flops 405832448 | bytes 8564814 | solution.py:106
  385.9 4.9 %conditional.7 = ((f32[256,3,128]{0,2,1:T(8,128)S(1)}, f32[256,3,128]{0,2,1:T(8,128)S(1)})) conditional(s32[]{:T(128)} %convert_element_type.71, (f32[256,3,128]{0,2,1:T(8,128)S(1)}, f32[256,3,128]{0,2,1:T(8,128)S(1)}) %tuple.108, (s32[]{:T(128)}, bf16[8192,3,128]{2,0,1:T(8,128)(2,1)}, s32[]{:T(128)}, bf16[256,3,128]{2,0,1:T(8,128)(2,1)S(1)}, ...), branch_computations={%region_7.7_spmd, %region_8.8_spmd} | conditional | flops 405832448 | bytes 8564814 | solution.py:106
  391.5 4.9 %conditional.7 = ((f32[256,3,128]{0,2,1:T(8,128)S(1)}, f32[256,3,128]{0,2,1:T(8,128)S(1)})) conditional(s32[]{:T(128)} %convert_element_type.71, (f32[256,3,128]{0,2,1:T(8,128)S(1)}, f32[256,3,128]{0,2,1:T(8,128)S(1)}) %tuple.108, (s32[]{:T(128)}, bf16[8192,3,128]{2,0,1:T(8,128)(2,1)}, s32[]{:T(128)}, bf16[256,3,128]{2,0,1:T(8,128)(2,1)S(1)}, ...), branch_computations={%region_7.7_spmd, %region_8.8_spmd} | conditional | flops 405832448 | bytes 8564814 | solution.py:106
  394.6 1.8 fusion.30
  397.1 4.9 %conditional.7 = ((f32[256,3,128]{0,2,1:T(8,128)S(1)}, f32[256,3,128]{0,2,1:T(8,128)S(1)})) conditional(s32[]{:T(128)} %convert_element_type.71, (f32[256,3,128]{0,2,1:T(8,128)S(1)}, f32[256,3,128]{0,2,1:T(8,128)S(1)}) %tuple.108, (s32[]{:T(128)}, bf16[8192,3,128]{2,0,1:T(8,128)(2,1)}, s32[]{:T(128)}, bf16[256,3,128]{2,0,1:T(8,128)(2,1)S(1)}, ...), branch_computations={%region_7.7_spmd, %region_8.8_spmd} | conditional | flops 405832448 | bytes 8564814 | solution.py:106
  402.6 4.9 %conditional.7 = ((f32[256,3,128]{0,2,1:T(8,128)S(1)}, f32[256,3,128]{0,2,1:T(8,128)S(1)})) conditional(s32[]{:T(128)} %convert_element_type.71, (f32[256,3,128]{0,2,1:T(8,128)S(1)}, f32[256,3,128]{0,2,1:T(8,128)S(1)}) %tuple.108, (s32[]{:T(128)}, bf16[8192,3,128]{2,0,1:T(8,128)(2,1)}, s32[]{:T(128)}, bf16[256,3,128]{2,0,1:T(8,128)(2,1)S(1)}, ...), branch_computations={%region_7.7_spmd, %region_8.8_spmd} | conditional | flops 405832448 | bytes 8564814 | solution.py:106
  405.8 1.8 fusion.30
  408.2 4.9 %conditional.7 = ((f32[256,3,128]{0,2,1:T(8,128)S(1)}, f32[256,3,128]{0,2,1:T(8,128)S(1)})) conditional(s32[]{:T(128)} %convert_element_type.71, (f32[256,3,128]{0,2,1:T(8,128)S(1)}, f32[256,3,128]{0,2,1:T(8,128)S(1)}) %tuple.108, (s32[]{:T(128)}, bf16[8192,3,128]{2,0,1:T(8,128)(2,1)}, s32[]{:T(128)}, bf16[256,3,128]{2,0,1:T(8,128)(2,1)S(1)}, ...), branch_computations={%region_7.7_spmd, %region_8.8_spmd} | conditional | flops 405832448 | bytes 8564814 | solution.py:106
  413.8 4.9 %conditional.7 = ((f32[256,3,128]{0,2,1:T(8,128)S(1)}, f32[256,3,128]{0,2,1:T(8,128)S(1)})) conditional(s32[]{:T(128)} %convert_element_type.71, (f32[256,3,128]{0,2,1:T(8,128)S(1)}, f32[256,3,128]{0,2,1:T(8,128)S(1)}) %tuple.108, (s32[]{:T(128)}, bf16[8192,3,128]{2,0,1:T(8,128)(2,1)}, s32[]{:T(128)}, bf16[256,3,128]{2,0,1:T(8,128)(2,1)S(1)}, ...), branch_computations={%region_7.7_spmd, %region_8.8_spmd} | conditional | flops 405832448 | bytes 8564814 | solution.py:106
  416.9 1.8 fusion.30
  419.4 4.9 %conditional.7 = ((f32[256,3,128]{0,2,1:T(8,128)S(1)}, f32[256,3,128]{0,2,1:T(8,128)S(1)})) conditional(s32[]{:T(128)} %convert_element_type.71, (f32[256,3,128]{0,2,1:T(8,128)S(1)}, f32[256,3,128]{0,2,1:T(8,128)S(1)}) %tuple.108, (s32[]{:T(128)}, bf16[8192,3,128]{2,0,1:T(8,128)(2,1)}, s32[]{:T(128)}, bf16[256,3,128]{2,0,1:T(8,128)(2,1)S(1)}, ...), branch_computations={%region_7.7_spmd, %region_8.8_spmd} | conditional | flops 405832448 | bytes 8564814 | solution.py:106
  425.0 4.9 %conditional.7 = ((f32[256,3,128]{0,2,1:T(8,128)S(1)}, f32[256,3,128]{0,2,1:T(8,128)S(1)})) conditional(s32[]{:T(128)} %convert_element_type.71, (f32[256,3,128]{0,2,1:T(8,128)S(1)}, f32[256,3,128]{0,2,1:T(8,128)S(1)}) %tuple.108, (s32[]{:T(128)}, bf16[8192,3,128]{2,0,1:T(8,128)(2,1)}, s32[]{:T(128)}, bf16[256,3,128]{2,0,1:T(8,128)(2,1)S(1)}, ...), branch_computations={%region_7.7_spmd, %region_8.8_spmd} | conditional | flops 405832448 | bytes 8564814 | solution.py:106
  430.6 4.9 %conditional.7 = ((f32[256,3,128]{0,2,1:T(8,128)S(1)}, f32[256,3,128]{0,2,1:T(8,128)S(1)})) conditional(s32[]{:T(128)} %convert_element_type.71, (f32[256,3,128]{0,2,1:T(8,128)S(1)}, f32[256,3,128]{0,2,1:T(8,128)S(1)}) %tuple.108, (s32[]{:T(128)}, bf16[8192,3,128]{2,0,1:T(8,128)(2,1)}, s32[]{:T(128)}, bf16[256,3,128]{2,0,1:T(8,128)(2,1)S(1)}, ...), branch_computations={%region_7.7_spmd, %region_8.8_spmd} | conditional | flops 405832448 | bytes 8564814 | solution.py:106
  436.2 4.9 %conditional.7 = ((f32[256,3,128]{0,2,1:T(8,128)S(1)}, f32[256,3,128]{0,2,1:T(8,128)S(1)})) conditional(s32[]{:T(128)} %convert_element_type.71, (f32[256,3,128]{0,2,1:T(8,128)S(1)}, f32[256,3,128]{0,2,1:T(8,128)S(1)}) %tuple.108, (s32[]{:T(128)}, bf16[8192,3,128]{2,0,1:T(8,128)(2,1)}, s32[]{:T(128)}, bf16[256,3,128]{2,0,1:T(8,128)(2,1)S(1)}, ...), branch_computations={%region_7.7_spmd, %region_8.8_spmd} | conditional | flops 405832448 | bytes 8564814 | solution.py:106
  441.8 4.9 %conditional.7 = ((f32[256,3,128]{0,2,1:T(8,128)S(1)}, f32[256,3,128]{0,2,1:T(8,128)S(1)})) conditional(s32[]{:T(128)} %convert_element_type.71, (f32[256,3,128]{0,2,1:T(8,128)S(1)}, f32[256,3,128]{0,2,1:T(8,128)S(1)}) %tuple.108, (s32[]{:T(128)}, bf16[8192,3,128]{2,0,1:T(8,128)(2,1)}, s32[]{:T(128)}, bf16[256,3,128]{2,0,1:T(8,128)(2,1)S(1)}, ...), branch_computations={%region_7.7_spmd, %region_8.8_spmd} | conditional | flops 405832448 | bytes 8564814 | solution.py:106
  447.3 4.9 %conditional.7 = ((f32[256,3,128]{0,2,1:T(8,128)S(1)}, f32[256,3,128]{0,2,1:T(8,128)S(1)})) conditional(s32[]{:T(128)} %convert_element_type.71, (f32[256,3,128]{0,2,1:T(8,128)S(1)}, f32[256,3,128]{0,2,1:T(8,128)S(1)}) %tuple.108, (s32[]{:T(128)}, bf16[8192,3,128]{2,0,1:T(8,128)(2,1)}, s32[]{:T(128)}, bf16[256,3,128]{2,0,1:T(8,128)(2,1)S(1)}, ...), branch_computations={%region_7.7_spmd, %region_8.8_spmd} | conditional | flops 405832448 | bytes 8564814 | solution.py:106
  452.9 4.9 %conditional.7 = ((f32[256,3,128]{0,2,1:T(8,128)S(1)}, f32[256,3,128]{0,2,1:T(8,128)S(1)})) conditional(s32[]{:T(128)} %convert_element_type.71, (f32[256,3,128]{0,2,1:T(8,128)S(1)}, f32[256,3,128]{0,2,1:T(8,128)S(1)}) %tuple.108, (s32[]{:T(128)}, bf16[8192,3,128]{2,0,1:T(8,128)(2,1)}, s32[]{:T(128)}, bf16[256,3,128]{2,0,1:T(8,128)(2,1)S(1)}, ...), branch_computations={%region_7.7_spmd, %region_8.8_spmd} | conditional | flops 405832448 | bytes 8564814 | solution.py:106
  (192 shorter events, 81.8 us)
Async XLA Ops:
  7.2 69.4 %all-gather.10.cloned.1.call-start = ((), (), s32[]{:S(2)}) async-start(), calls=%async_computation.2 | async-start | bytes 2949120 | tf_op jit(solution)/shard_map/all_gather | solution.py:123
  7.9 145.1 %all-gather.6.cloned.1.call-start = ((), (), s32[]{:S(2)}) async-start(), calls=%async_computation | async-start | bytes 6488064 | tf_op jit(solution)/shard_map/all_gather | solution.py:135
  8.6 208.7 %all-gather.8.cloned.1.call-start = ((), (), s32[]{:S(2)}) async-start(), calls=%async_computation.1 | async-start | bytes 6488064 | tf_op jit(solution)/shard_map/all_gather | solution.py:136
  9.4 74.4 %copy-start.4 = (f32[256,3]{0,1:T(4,128)S(1)}, f32[256,3]{0,1:T(4,128)}, u32[]{:S(2)}) copy-start(f32[256,3]{0,1:T(4,128)} %param.21) | copy-start | bytes 9220
  9.4 289.7 %all-gather.14.cloned.1.call-start = ((), (), s32[]{:S(2)}) async-start(), calls=%async_computation.4 | async-start | bytes 6488064 | tf_op jit(solution)/shard_map/all_gather | solution.py:144
  81.0 40.6 %copy-start.3 = (bf16[256,3,128]{2,0,1:T(8,128)(2,1)S(1)}, bf16[256,3,128]{2,0,1:T(8,128)(2,1)}, u32[]{:S(2)}) copy-start(bf16[256,3,128]{2,0,1:T(8,128)(2,1)} %param.18) | copy-start | bytes 589828
  81.0 136.4 %copy-start = (bf16[256,3,128]{2,0,1:T(8,128)(2,1)S(1)}, bf16[256,3,128]{2,0,1:T(8,128)(2,1)}, u32[]{:S(2)}) copy-start(bf16[256,3,128]{2,0,1:T(8,128)(2,1)} %param.15) | copy-start | bytes 589828
  81.9 286.5 %all-gather.12.cloned.1.call-start = ((), (), s32[]{:S(2)}) async-start(), calls=%async_computation.3 | async-start | bytes 6488064 | tf_op jit(solution)/shard_map/all_gather | solution.py:143
  232.9 135.6 %copy-start.1 = (bf16[256,3,128]{2,0,1:T(8,128)(2,1)S(1)}, bf16[256,3,128]{2,0,1:T(8,128)(2,1)}, u32[]{:S(2)}) copy-start(bf16[256,3,128]{2,0,1:T(8,128)(2,1)} %param.17) | copy-start | bytes 589828
  232.9 135.6 %copy-start.2 = (bf16[256,3,128]{2,0,1:T(8,128)(2,1)S(1)}, bf16[256,3,128]{2,0,1:T(8,128)(2,1)}, u32[]{:S(2)}) copy-start(bf16[256,3,128]{2,0,1:T(8,128)(2,1)} %param.16) | copy-start | bytes 589828
Sparse Core Ops, SparseCore 0:
  10.7 65.8 all-gather.9
  78.5 68.2 all-gather.5
  148.6 68.7 all-gather.7
  219.6 79.4 all-gather.13
  300.8 67.5 all-gather.11
where the time goes:
time: 468 us; the launch traced here: 466 us
  waiting for transfers between devices  261 us (56%)
  matrix products  82.6 us (18%)
  blocking collectives  66.8 us (14%)
  loops' own time  23 us (5%)
  local copies, waits for them, and re-layouts  14.4 us (3%)
  between operations  13.9 us (3%)
    all_gather x1, waiting for transfers between devices, body(): lax.all_gather(output_grad, 'head', axis=1, tiled=True)  67.1 us
    all_gather x1, waiting for transfers between devices, body(): lax.all_gather(attn_grad, 'ctx', axis=0, tiled=True)  66.2 us
    all_gather x1, waiting for transfers between devices, body(): lax.all_gather(value_vectors, 'ctx', axis=0, tiled=True)  64.4 us
    all_gather x1, waiting for transfers between devices, body(): lax.all_gather(queries, 'ctx', axis=0, tiled=True)  60.7 us
    all_gather x1, blocking collectives, body(): lax.all_gather(own_total, 'ctx', axis=1, tiled=True)  35.6 us
    all_gather x1, blocking collectives, body(): lax.all_gather(row_delta, 'ctx', axis=1, tiled=True)  31.2 us
    dot_general x16, matrix products, key_update(): jnp.einsum('hqk,qhd->khd', score_grad, query_block, preferred_element_typ...  28.6 us
    dot_general x17, matrix products, block_terms(): jnp.einsum('qhd,khd->hqk', query_block, key_block, preferred_element_type...  25.9 us
  transfers between devices with their start and end apart: 5, of which 4 were waited for; matrix products, arithmetic and copies ran while one was open for 5% of the time, Pallas kernels for 0%

commit v1 on v0

v1 whole, which is shorter than its diff:
```python
import functools
import math

import jax
import jax.numpy as jnp
from jax import lax
from jax.experimental import pallas as pl
from jax.experimental.pallas import tpu as pltpu
from jax.sharding import PartitionSpec as P

MESH = pl.DeviceIdType.MESH
BF = jnp.bfloat16
F32 = jnp.float32
LOG2E = math.log2(math.e)
Z = 8
Y = 4

NT = (((1,), (1,)), ((), ()))
TN = (((0,), (0,)), ((), ()))
NN = (((1,), (0,)), ((), ()))


def mm(a, b, dims):
    return lax.dot_general(a, b, dims, preferred_element_type=F32)


def kernel(
    q_ref, k_ref, v_ref, o_ref, g_ref, lse_ref, w_hbm,
    dq_out, dk_out, dv_out,
    w_vm, gall, qall, kall, vall, doall, stat, dqb, sbuf, rbuf, rown,
    dkacc, dvacc, dq0, kv1s, kv1r, kv2s, kv2r,
    w_sem, send_sem, recv_sem,
):
    heads, rows, width = q_ref.shape
    half = rows // 2
    factor = width ** -0.5
    ctx = lax.axis_index("ctx")
    hd = lax.axis_index("head")
    z = ctx // 4
    p = ctx % 4
    xb, cb = p // 2, p % 2
    xh, y = hd // Y, hd % Y

    up = ((z + 1) % Z * 4 + p, hd)
    down = ((z + Z - 1) % Z * 4 + p, hd)
    north = (ctx, xh * Y + (y + 1) % Y)
    south = (ctx, xh * Y + (y + Y - 1) % Y)
    across = (ctx, (1 - xh) * Y + y)
    side = (z * 4 + (1 - xb) * 2 + cb, hd)
    twin = (z * 4 + xb * 2 + 1 - cb, hd)
    peers = (up, down, north, south, across, side, twin)

    counter = [0]

    def copy(src, dst, to):
        n = counter[0]
        counter[0] += 1
        return pltpu.make_async_remote_copy(
            src_ref=src, dst_ref=dst, send_sem=send_sem.at[n], recv_sem=recv_sem.at[n],
            device_id=to, device_id_type=MESH)

    wcopy = pltpu.make_async_copy(w_hbm, w_vm, w_sem)
    wcopy.start()

    barrier = pltpu.get_barrier_semaphore()
    for peer in peers:
        pl.semaphore_signal(barrier, inc=1, device_id=peer, device_id_type=MESH)
    pl.semaphore_wait(barrier, len(peers))

    started = []

    def go(src, dst, to):
        c = copy(src, dst, to)
        c.start()
        started.append(c)
        return c

    g01 = go(g_ref, gall.at[0, 1], south)
    g03 = go(g_ref, gall.at[0, 3], north)
    g10 = go(g_ref, gall.at[1, 0], across)
    q1 = go(q_ref, qall.at[1], down)
    q7 = go(q_ref, qall.at[7], up)
    k2 = go(k_ref, kall.at[:, 2], side)
    v2 = go(v_ref, vall.at[:, 2], side)
    k1 = go(k_ref, kall.at[:, 1], twin)
    v1 = go(v_ref, vall.at[:, 1], twin)

    qall[0] = q_ref[...]
    kall[:, 0] = k_ref[...]
    vall[:, 0] = v_ref[...]
    dqb[...] = jnp.zeros_like(dqb)
    dkacc[...] = jnp.zeros_like(dkacc)
    dvacc[...] = jnp.zeros_like(dvacc)
    wcopy.wait()

    def columns(a, b):
        at = ((xh + a) % 2 * Y + (y + b) % Y) * g_ref.shape[1]
        return pl.ds(pl.multiple_of(at, 128), g_ref.shape[1])

    def proj(a, b, block):
        return mm(block, w_vm[:, columns(a, b)], NT)

    acc = proj(0, 0, g_ref[...])

    q1.wait_recv()
    q2 = go(qall.at[1], qall.at[2], down)
    q7.wait_recv()
    q6 = go(qall.at[7], qall.at[6], up)
    g01.wait_recv()
    g02a = go(gall.at[0, 1, pl.ds(0, half)], gall.at[0, 2, pl.ds(0, half)], south)
    g03.wait_recv()
    g02b = go(gall.at[0, 3, pl.ds(half, half)], gall.at[0, 2, pl.ds(half, half)], north)
    acc += proj(0, 1, gall[0, 1])
    acc += proj(0, 3, gall[0, 3])
    q2.wait_recv()
    q3 = go(qall.at[2], qall.at[3], down)
    q6.wait_recv()
    q5 = go(qall.at[6], qall.at[5], up)
    g10.wait_recv()
    g11 = go(gall.at[1, 0], gall.at[1, 1], south)
    g13 = go(gall.at[1, 0], gall.at[1, 3], north)
    acc += proj(1, 0, gall[1, 0])
    k2.wait_recv()
    k3 = go(kall.at[:, 2], kall.at[:, 3], twin)
    v2.wait_recv()
    v3 = go(vall.at[:, 2], vall.at[:, 3], twin)
    q3.wait_recv()
    q4a = go(qall.at[3, :, pl.ds(0, half)], qall.at[4, :, pl.ds(0, half)], down)
    q5.wait_recv()
    q4b = go(qall.at[5, :, pl.ds(half, half)], qall.at[4, :, pl.ds(half, half)], up)
    g02a.wait_recv()
    g02b.wait_recv()
    acc += proj(0, 2, gall[0, 2])
    g11.wait_recv()
    g12a = go(gall.at[1, 1, pl.ds(0, half)], gall.at[1, 2, pl.ds(0, half)], south)
    g13.wait_recv()
    g12b = go(gall.at[1, 3, pl.ds(half, half)], gall.at[1, 2, pl.ds(half, half)], north)
    acc += proj(1, 1, gall[1, 1])
    acc += proj(1, 3, gall[1, 3])
    k1.wait_recv()
    v1.wait_recv()
    k3.wait_recv()
    v3.wait_recv()
    q4a.wait_recv()
    q4b.wait_recv()
    g12a.wait_recv()
    g12b.wait_recv()
    acc += proj(1, 2, gall[1, 2])

    grad = acc.astype(BF)
    stat[0] = jnp.zeros(stat.shape[1:], F32)
    for h in range(heads):
        grad_h = grad[:, h * width:(h + 1) * width]
        doall[0, h] = grad_h
        terms = grad_h.astype(F32) * o_ref[h].astype(F32)
        delta = jnp.sum(terms, axis=1, keepdims=True)
        stat[0, heads + h:heads + h + 1, :] = jnp.transpose(
            jnp.broadcast_to(delta, (rows, 128)), (1, 0))[0:1, :]
    stat[0, 0:heads, :] = lse_ref[...] * LOG2E

    d1 = go(doall.at[0], doall.at[1], down)
    s1 = go(stat.at[0], stat.at[1], down)
    d7 = go(doall.at[0], doall.at[7], up)
    s7 = go(stat.at[0], stat.at[7], up)

    def process(r, masked=False):
        def one(h, carry):
            keys = kall[h].reshape(4 * rows, width)
            values = vall[h].reshape(4 * rows, width)
            query = qall[r, h]
            grad = doall[r, h]
            total = stat[r, pl.ds(h, 1), :]
            delta = stat[r, pl.ds(heads + h, 1), :]
            raw = mm(keys, query, NT)
            shifted = raw * (factor * LOG2E) - total
            if masked:
                row = lax.broadcasted_iota(jnp.int32, shifted.shape, 0)
                col = lax.broadcasted_iota(jnp.int32, shifted.shape, 1)
                offs = []
                for j in range(4):
                    jx, jc = j // 2, j % 2
                    pj = (xb + jx) % 2 * 2 + (cb + jc) % 2
                    offs.append((pj - p - j) * rows)
                off = jnp.where(
                    row < 2 * rows,
                    jnp.where(row < rows, offs[0], offs[1]),
                    jnp.where(row < 3 * rows, offs[2], offs[3]))
                shifted = jnp.where(row + off <= col, shifted, -jnp.inf)
            prob = jnp.exp2(shifted)
            pgrad = mm(values, grad, NT)
            score = (prob * (pgrad - delta)).astype(BF)
            dvacc[h] += mm(prob.astype(BF), grad, NN)
            dkacc[h] += mm(score, query, NN)
            part = mm(score, keys, TN)
            if r == 0:
                dq0[h] = part
            else:
                dqb[r, h] = part.astype(BF)
            return carry

        lax.fori_loop(0, heads, one, 0)

    def guarded(r):
        @pl.when(z + r < Z)
        def _():
            process(r)

    process(0, masked=True)
    d1.wait_recv()
    d2 = go(doall.at[1], doall.at[2], down)
    s1.wait_recv()
    s2 = go(stat.at[1], stat.at[2], down)
    d7.wait_recv()
    d6 = go(doall.at[7], doall.at[6], up)
    s7.wait_recv()
    s6 = go(stat.at[7], stat.at[6], up)
    guarded(1)
    d2.wait_recv()
    d3 = go(doall.at[2], doall.at[3], down)
    s2.wait_recv()
    s3 = go(stat.at[2], stat.at[3], down)
    d6.wait_recv()
    d5 = go(doall.at[6], doall.at[5], up)
    s6.wait_recv()
    s5 = go(stat.at[6], stat.at[5], up)
    guarded(2)
    d3.wait_recv()
    d4a = go(doall.at[3, :, pl.ds(0, half)], doall.at[4, :, pl.ds(0, half)], down)
    s3.wait_recv()
    s4 = go(stat.at[3], stat.at[4], down)
    d5.wait_recv()
    d4b = go(doall.at[5, :, pl.ds(half, half)], doall.at[4, :, pl.ds(half, half)], up)
    s5.wait_recv()
    guarded(3)
    d4a.wait_recv()
    d4b.wait_recv()
    s4.wait_recv()
    guarded(4)

    def plus(a, b):
        return (a.astype(F32) + b.astype(F32)).astype(BF)

    lo, hi = pl.ds(0, half), pl.ds(half, half)
    r3 = go(dqb.at[4, :, lo], rbuf.at[3, :, lo], up)
    r5 = go(dqb.at[4, :, hi], rbuf.at[5, :, hi], down)
    guarded(5)
    r3.wait_recv()
    sbuf[3, :, :half] = plus(dqb[3, :, :half], rbuf[3, :, :half])
    sbuf[3, :, half:] = dqb[3, :, half:]
    r2 = go(sbuf.at[3], rbuf.at[2], up)
    r5.wait_recv()
    sbuf[5, :, half:] = plus(dqb[5, :, half:], rbuf[5, :, half:])
    sbuf[5, :, :half] = dqb[5, :, :half]
    r6 = go(sbuf.at[5], rbuf.at[6], down)
    guarded(6)
    r2.wait_recv()
    sbuf[2] = plus(dqb[2], rbuf[2])
    r1 = go(sbuf.at[2], rbuf.at[1], up)
    r6.wait_recv()
    sbuf[6] = plus(dqb[6], rbuf[6])
    r7 = go(sbuf.at[6], rbuf.at[7], down)
    guarded(7)

    for j, slot in ((0, 1), (1, 3)):
        at = pl.ds(slot * rows, rows)
        kv1s[j, 0] = dkacc[:, at, :].astype(BF)
        kv1s[j, 1] = dvacc[:, at, :].astype(BF)
    t1 = go(kv1s, kv1r, twin)
    r1.wait_recv()
    sbuf[1] = plus(dqb[1], rbuf[1])
    r0 = go(sbuf.at[1], rown.at[0], up)
    r7.wait_recv()
    sbuf[7] = plus(dqb[7], rbuf[7])
    r8 = go(sbuf.at[7], rown.at[1], down)
    t1.wait_recv()
    at = pl.ds(2 * rows, rows)
    kv2s[0] = (dkacc[:, at, :] + kv1r[1, 0].astype(F32)).astype(BF)
    kv2s[1] = (dvacc[:, at, :] + kv1r[1, 1].astype(F32)).astype(BF)
    t2 = go(kv2s, kv2r, side)
    at = pl.ds(0, rows)
    key_sum = dkacc[:, at, :] + kv1r[0, 0].astype(F32)
    value_sum = dvacc[:, at, :] + kv1r[0, 1].astype(F32)
    t2.wait_recv()
    dk_out[...] = ((key_sum + kv2r[0].astype(F32)) * factor).astype(BF)
    dv_out[...] = (value_sum + kv2r[1].astype(F32)).astype(BF)
    r0.wait_recv()
    r8.wait_recv()
    dq_out[...] = ((dq0[...] + rown[0].astype(F32) + rown[1].astype(F32)) * factor).astype(BF)

    for c in started:
        c.wait_send()


COPIES = 64


def body(queries, key_vectors, value_vectors, attn_output, output_grad, w_out, log_total):
    rows, heads, width = queries.shape
    major = lambda a: jnp.transpose(a, (1, 0, 2))
    block = jax.ShapeDtypeStruct((heads, rows, width), BF)
    vmem = pl.BlockSpec(memory_space=pltpu.VMEM)
    V = pltpu.VMEM
    blk = (heads, rows, width)
    outs = pl.pallas_call(
        kernel,
        out_shape=(block, block, block),
        in_specs=[vmem] * 6 + [pl.BlockSpec(memory_space=pl.ANY)],
        out_specs=(vmem, vmem, vmem),
        scratch_shapes=[
            V(w_out.shape, BF),
            V((2, Y) + output_grad.shape, BF),
            V((Z,) + blk, BF),
            V((heads, 4, rows, width), BF),
            V((heads, 4, rows, width), BF),
            V((Z,) + blk, BF),
            V((Z, 8, rows), F32),
            V((Z,) + blk, BF),
            V((Z,) + blk, BF),
            V((Z,) + blk, BF),
            V((2,) + blk, BF),
            V((heads, 4 * rows, width), F32),
            V((heads, 4 * rows, width), F32),
            V(blk, F32),
            V((2, 2) + blk, BF),
            V((2, 2) + blk, BF),
            V((2,) + blk, BF),
            V((2,) + blk, BF),
            pltpu.SemaphoreType.DMA,
            pltpu.SemaphoreType.DMA((COPIES,)),
            pltpu.SemaphoreType.DMA((COPIES,)),
        ],
        compiler_params=pltpu.CompilerParams(
            collective_id=0, has_side_effects=True, vmem_limit_bytes=60 * 1024 * 1024),
        name="attention_backward",
    )(
        major(queries), major(key_vectors), major(value_vectors), major(attn_output),
        output_grad, jnp.transpose(log_total, (1, 0)), w_out,
    )
    return tuple(major(a) for a in outs)


def solution(mesh):
    row = P("ctx", "head", None)
    return jax.shard_map(
        body, mesh=mesh,
        in_specs=(row, row, row, row, P("ctx", "head"), P("head", None), P("ctx", "head")),
        out_specs=(row, row, row), check_vma=False)
```

time: 468 us -> 94.6 us (0.20)
  waiting for transfers between devices: 261 us -> 0 us
  Pallas kernels: 0 us -> 88.9 us
  matrix products: 82.6 us -> 0 us
  blocking collectives: 66.8 us -> 0 us
  loops' own time: 23 us -> 0 us
  between operations: 13.9 us -> 0.64 us
  local copies, waits for them, and re-layouts: 14.4 us -> 4.85 us
    all_gather x5 -> x0, waiting for transfers between devices: 258 us -> none  [the longest x1 67.1 us: body(): lax.all_gather(output_grad, 'head', axis=1, tiled=True)]
    pallas_call x0 -> x1, Pallas kernels: none -> 88.9 us  [body(): pl.pallas_call(kernel, out_shape=(block, block, block), in_specs=[vmem] *...]
    dot_general x51 -> x0, matrix products: 82.6 us -> none  [the longest x16 28.6 us: key_update(): jnp.einsum('hqk,qhd->khd', score_grad, query_block, preferred_element_typ...]
    all_gather x2 -> x0, blocking collectives: 66.8 us -> none  [the longest x1 35.6 us: body(): lax.all_gather(own_total, 'ctx', axis=1, tiled=True)]
    another operation x34 -> x0, loops' own time: 23 us -> none  [the longest x1 10.9 us: query_pass(): lax.fori_loop(0, gathered_keys.shape[0] // span_rows, query_advance, init...]
    unnamed x13 -> x3, local copies, waits for them, and re-layouts: 10.8 us -> 4.85 us
  transfers between devices with their start and end apart: 5 -> 0, of which waited for: 4 -> 0; matrix products, arithmetic and copies ran while one was open for 5% -> 0% of each run, Pallas kernels for 0% -> 0%
where the time goes in v1:
time: 94.6 us; the launch traced here: 94.4 us
  Pallas kernels  88.9 us (94%)
  local copies, waits for them, and re-layouts  4.85 us (5%)
    pallas_call x1, Pallas kernels, body(): pl.pallas_call(kernel, out_shape=(block, block, block), in_specs=[vmem] *...  88.9 us
    unnamed x3, local copies, waits for them, and re-layouts  4.85 us

profile of v1, /device:TPU:1, one launch (start us, length us, event | category | flops | bytes accessed | tf_op | source)
XLA Modules:
  0.0 94.4 jit_solution(9446240700322122683)
XLA Ops:
  0.6 88.9 %attention_backward.1 = (bf16[3,256,128]{2,1,0:T(8,128)(2,1)}, bf16[3,256,128]{2,1,0:T(8,128)(2,1)}, bf16[3,256,128]{2,1,0:T(8,128)(2,1)}) custom-call(bf16[3,256,128]{2,1,0:T(8,128)(2,1)} %bitcast.8, bf16[3,256,128]{2,1,0:T(8,128)(2,1)} %bitcast.9, bf16[3,256,128]{2,1,0:T(8,128)(2,1)} %bitcast.10, bf16[3,256,128]{2,1,0:T(8,128)(2,1)} %bitcast.11, ...), custom_call_target="tpu_custom_call" | custom-call | tf_op jit(solution)/shard_map/attention_backward/pallas_call | solution.py:304
  89.6 1.6 %copy.13 = bf16[256,3,128]{2,0,1:T(8,128)(2,1)} copy(bf16[256,3,128]{2,0,1:T(8,128)(2,1)} %bitcast.14) | data formatting | bytes 393216
  91.2 1.6 %copy.14 = bf16[256,3,128]{2,0,1:T(8,128)(2,1)} copy(bf16[256,3,128]{2,0,1:T(8,128)(2,1)} %bitcast.13) | data formatting | bytes 393216
  92.8 1.6 %copy.15 = bf16[256,3,128]{2,0,1:T(8,128)(2,1)} copy(bf16[256,3,128]{2,0,1:T(8,128)(2,1)} %bitcast.12) | data formatting | bytes 393216

commit v2 on v1

v2 whole, which is shorter than its diff:
```python
import math

import jax
import jax.numpy as jnp
from jax import lax
from jax.experimental import pallas as pl
from jax.experimental.pallas import tpu as pltpu
from jax.sharding import PartitionSpec as P

MESH = pl.DeviceIdType.MESH
BF = jnp.bfloat16
F32 = jnp.float32
LOG2E = math.log2(math.e)
Z = 8
Y = 4
COPIES = 160

NT = (((1,), (1,)), ((), ()))
TN = (((0,), (0,)), ((), ()))
NN = (((1,), (0,)), ((), ()))


def mm(a, b, dims):
    return lax.dot_general(a, b, dims, preferred_element_type=F32)


def plus(a, b):
    return (a.astype(F32) + b.astype(F32)).astype(BF)


def kernel(
    q_ref, k_ref, v_ref, o_ref, g_ref, lse_ref, w_hbm,
    dq_out, dk_out, dv_out,
    w_vm, gall, qall, kall, vall, doall, stat, dqb, sbuf, rbuf, rown,
    dkacc, dvacc, dq0, kv1s, kv1r, kv2s, kv2r,
    w_sem, send_sem, recv_sem,
):
    heads, rows, width = q_ref.shape
    half = rows // 2
    factor = width ** -0.5
    ctx = lax.axis_index("ctx")
    hd = lax.axis_index("head")
    z = ctx // 4
    p = ctx % 4
    xb, cb = p // 2, p % 2
    xh, y = hd // Y, hd % Y

    def plane(to):
        return ((to + Z) % Z * 4 + p, hd)

    up, down = plane(z + 1), plane(z - 1)
    north = (ctx, xh * Y + (y + 1) % Y)
    south = (ctx, xh * Y + (y + Y - 1) % Y)
    across = (ctx, (1 - xh) * Y + y)
    side = (z * 4 + (1 - xb) * 2 + cb, hd)
    twin = (z * 4 + xb * 2 + 1 - cb, hd)
    peers = [plane(z + d) for d in (-3, -2, -1, 1, 2, 3)]
    peers += [north, south, across, side, twin]

    wcopy = pltpu.make_async_copy(w_hbm, w_vm, w_sem)
    wcopy.start()
    barrier = pltpu.get_barrier_semaphore()
    for peer in peers:
        pl.semaphore_signal(barrier, inc=1, device_id=peer, device_id_type=MESH)

    used = [0]
    channels = []

    def when(cond, act):
        if cond is None:
            act()
        else:
            pl.when(cond)(act)

    class Channel:
        def __init__(self, src, dst, to, send_if=None, recv_if=None, n=heads, shift=0, slots=None):
            self.src, self.dst, self.to, self.shift = src, dst, to, shift
            self.send_if, self.recv_if, self.n = send_if, recv_if, n
            self.base = used[0]
            used[0] += slots or n
            channels.append(self)

        def copy(self, i, shift):
            at = self.base + shift + i
            return pltpu.make_async_remote_copy(
                src_ref=self.src(i), dst_ref=self.dst(i),
                send_sem=send_sem.at[at], recv_sem=recv_sem.at[at],
                device_id=self.to, device_id_type=MESH)

        def start(self, i=0):
            when(self.send_if, lambda: self.copy(i, self.shift).start())

        def recv(self, i=0):
            when(self.recv_if, lambda: self.copy(i, 0).wait_recv())

        def recv_at(self, i, shift, cond):
            when(cond, lambda: self.copy(i, shift).wait_recv())

        def drain(self):
            def act():
                for i in range(self.n):
                    self.copy(i, self.shift).wait_send()
            when(self.send_if, act)

    def once(src, dst, to, **kw):
        return Channel(lambda i: src, lambda i: dst, to, n=1, **kw)

    def valid(r):
        return z + r <= Z - 1

    class Ring:
        def __init__(self, own, held, n):
            self.hops = {}
            for r in range(1, 5):
                src = own if r == 1 else (lambda i, r=r: held(r - 1, i))
                self.hops[r] = Channel(
                    src, lambda i, r=r: held(r, i), down, n=n,
                    send_if=(z >= 1) & (z - 1 + r <= Z - 1), recv_if=valid(r))
            self.wrap = Channel(
                own, lambda i: held(z, i), plane(0), n=n, send_if=z >= 5,
                shift=(z - 5) * n, slots=3 * n)
            self.seven = Channel(
                lambda i: held(7, i), lambda i: held(6, i), up, n=n,
                send_if=z == 0, recv_if=z == 1)
            self.six = Channel(
                lambda i: held(6, i), lambda i: held(5, i), up, n=n,
                send_if=z <= 1, recv_if=(z == 1) | (z == 2))
            self.n = n

        def begin(self):
            for i in range(self.n):
                self.hops[1].start(i)
                self.wrap.start(i)

        def recv(self, r, i):
            if r <= 4:
                self.hops[r].recv(i)
            else:
                self.wrap.recv_at(i, (r - 5) * self.n, z == 0)
                if r == 6:
                    self.seven.recv(i)
                if r == 5:
                    self.six.recv(i)

        def pass_on(self, r, i):
            if r < 4:
                self.hops[r + 1].start(i)
            if r == 7:
                self.seven.start(i)
            if r == 6:
                self.six.start(i)

    lo, hi = pl.ds(0, half), pl.ds(half, half)
    quarter = half // 2
    q_lo, q_mid = pl.ds(0, quarter), pl.ds(quarter, quarter)
    q_mid2, q_hi = pl.ds(half, quarter), pl.ds(half + quarter, quarter)

    g01 = [once(g_ref.at[s], gall.at[0, 1, s], south) for s in (lo, hi)]
    g03 = [once(g_ref.at[s], gall.at[0, 3, s], north) for s in (lo, hi)]
    g10 = [once(g_ref.at[s], gall.at[1, 0, s], across) for s in (lo, hi)]
    g02 = [once(gall.at[0, 1, lo], gall.at[0, 2, lo], south),
           once(gall.at[0, 3, hi], gall.at[0, 2, hi], north)]
    g11 = [once(gall.at[1, 0, s], gall.at[1, 1, s], south) for s in (lo, hi)]
    g13 = [once(gall.at[1, 0, s], gall.at[1, 3, s], north) for s in (lo, hi)]
    g12 = [once(gall.at[1, 1, q_lo], gall.at[1, 2, q_lo], south),
           once(gall.at[1, 3, q_hi], gall.at[1, 2, q_hi], north),
           once(gall.at[0, 2, q_mid], gall.at[1, 2, q_mid], across),
           once(gall.at[0, 2, q_mid2], gall.at[1, 2, q_mid2], across)]
    qring = Ring(lambda i: q_ref.at[i], lambda r, i: qall.at[r, i], heads)
    k2 = once(k_ref, kall.at[:, 2], side)
    v2 = once(v_ref, vall.at[:, 2], side)
    k1 = once(k_ref, kall.at[:, 1], twin)
    v1 = once(v_ref, vall.at[:, 1], twin)
    k3 = once(kall.at[:, 2], kall.at[:, 3], twin)
    v3 = once(vall.at[:, 2], vall.at[:, 3], twin)

    dkacc[...] = jnp.zeros_like(dkacc)
    dvacc[...] = jnp.zeros_like(dvacc)
    qall[0] = q_ref[...]
    kall[:, 0] = k_ref[...]
    vall[:, 0] = v_ref[...]
    pl.semaphore_wait(barrier, len(peers))

    g01[0].start()
    g03[1].start()
    g10[0].start()
    qring.begin()
    g01[1].start()
    g03[0].start()
    g10[1].start()
    k2.start()
    v2.start()
    k1.start()
    v1.start()
    wcopy.wait()

    def proj(a, b, block):
        at = ((xh + a) % 2 * Y + (y + b) % Y) * g_ref.shape[1]
        return mm(block, w_vm[:, pl.ds(pl.multiple_of(at, 128), g_ref.shape[1])], NT)

    acc = proj(0, 0, g_ref[...])
    for i in range(heads):
        qring.recv(1, i)
        qring.pass_on(1, i)
        if i == 1:
            g01[0].recv()
            g02[0].start()
            g03[1].recv()
            g02[1].start()
    g10[0].recv()
    g11[0].start()
    g13[0].start()
    for i in range(heads):
        qring.recv(2, i)
        qring.pass_on(2, i)
        qring.recv(7, i)
        qring.pass_on(7, i)
        if i == 1:
            g10[1].recv()
            g13[1].start()
            g11[1].start()
    g01[1].recv()
    g03[0].recv()
    acc += proj(0, 1, gall[0, 1])
    acc += proj(0, 3, gall[0, 3])
    acc += proj(1, 0, gall[1, 0])
    g02[0].recv()
    g12[2].start()
    g02[1].recv()
    g12[3].start()
    for i in range(heads):
        qring.recv(3, i)
        qring.pass_on(3, i)
        qring.recv(6, i)
        qring.pass_on(6, i)
    k2.recv()
    k3.start()
    v2.recv()
    v3.start()
    acc += proj(0, 2, gall[0, 2])
    g11[0].recv()
    g12[0].start()
    g13[1].recv()
    g12[1].start()
    g11[1].recv()
    g13[0].recv()
    acc += proj(1, 1, gall[1, 1])
    acc += proj(1, 3, gall[1, 3])
    for i in range(heads):
        qring.recv(4, i)
        qring.recv(5, i)
    k1.recv()
    v1.recv()
    k3.recv()
    v3.recv()
    for c in g12:
        c.recv()
    acc += proj(1, 2, gall[1, 2])

    grad = acc.astype(BF)
    stat[0] = jnp.zeros(stat.shape[1:], F32)
    for h in range(heads):
        grad_h = grad[:, h * width:(h + 1) * width]
        doall[0, h] = grad_h
        terms = grad_h.astype(F32) * o_ref[h].astype(F32)
        delta = jnp.sum(terms, axis=1, keepdims=True)
        stat[0, heads + h:heads + h + 1, :] = jnp.transpose(
            jnp.broadcast_to(delta, (rows, 128)), (1, 0))[0:1, :]
    stat[0, 0:heads, :] = lse_ref[...] * LOG2E

    sring = Ring(lambda i: stat.at[0], lambda r, i: stat.at[r], 1)
    dring = Ring(lambda i: doall.at[0, i], lambda r, i: doall.at[r, i], heads)
    sring.begin()
    dring.begin()

    def tile(r, h, masked=False):
        keys = kall[h].reshape(4 * rows, width)
        values = vall[h].reshape(4 * rows, width)
        query = qall[r, h]
        grad = doall[r, h]
        total = stat[r, pl.ds(h, 1), :]
        delta = stat[r, pl.ds(heads + h, 1), :]
        raw = mm(keys, query, NT)
        shifted = raw * (factor * LOG2E) - total
        if masked:
            row = lax.broadcasted_iota(jnp.int32, shifted.shape, 0)
            col = lax.broadcasted_iota(jnp.int32, shifted.shape, 1)
            offs = []
            for j in range(4):
                jx, jc = j // 2, j % 2
                pj = (xb + jx) % 2 * 2 + (cb + jc) % 2
                offs.append((pj - p - j) * rows)
            off = jnp.where(
                row < 2 * rows,
                jnp.where(row < rows, offs[0], offs[1]),
                jnp.where(row < 3 * rows, offs[2], offs[3]))
            shifted = jnp.where(row + off <= col, shifted, -jnp.inf)
        prob = jnp.exp2(shifted)
        pgrad = mm(values, grad, NT)
        score = (prob * (pgrad - delta)).astype(BF)
        dvacc[h] += mm(prob.astype(BF), grad, NN)
        dkacc[h] += mm(score, query, NN)
        part = mm(score, keys, TN)
        if r == 0:
            dq0[h] = part
        else:
            dqb[r, h] = part.astype(BF)

    def each(act):
        def one(h, carry):
            act(h)
            return carry
        lax.fori_loop(0, heads, one, 0)

    def take(r, h):
        if isinstance(h, int):
            first = h == 0
            if first:
                sring.recv(r, 0)
                sring.pass_on(r, 0)
        else:
            @pl.when(h == 0)
            def _():
                sring.recv(r, 0)
                sring.pass_on(r, 0)
        dring.recv(r, h)
        dring.pass_on(r, h)

    def guarded(r, h):
        pl.when(valid(r))(lambda: tile(r, h))

    part = lambda r: (lambda i: dqb.at[r, i])
    r2 = Channel(part(2), lambda i: rbuf.at[1, i], up, send_if=valid(2), recv_if=(z >= 1) & valid(1))
    r1 = Channel(lambda i: sbuf.at[1, i], lambda i: rown.at[1, i], up, send_if=valid(1), recv_if=z >= 1)
    r4 = Channel(part(4), lambda i: rbuf.at[3, i], up, send_if=valid(4), recv_if=(z >= 1) & valid(3))
    r3 = Channel(lambda i: sbuf.at[3, i], lambda i: rown.at[0, i], plane(z + 3), send_if=valid(3), recv_if=z >= 3)
    r5 = Channel(part(5), lambda i: rbuf.at[6, i], down, send_if=(z >= 1) & valid(5), recv_if=z <= 1)
    r6 = Channel(lambda i: sbuf.at[6, i], lambda i: rbuf.at[7, i], down, send_if=z == 1, recv_if=z == 0)
    last = {
        r: Channel(src, lambda i: rown.at[2, i], plane(r), send_if=z == 0, recv_if=z == r)
        for r, src in ((5, part(5)), (6, lambda i: sbuf.at[6, i]), (7, lambda i: sbuf.at[7, i]))
    }
    t1 = Channel(lambda i: kv1s.at[i], lambda i: kv1r.at[i], twin)
    t2 = Channel(lambda i: kv2s.at[i], lambda i: kv2r.at[i], side)

    each(lambda h: tile(0, h, masked=True))

    def stage1(h):
        take(1, h)
        guarded(1, h)

    each(stage1)

    def stage7(h):
        take(7, h)
        guarded(7, h)

    each(stage7)

    def stage2(h):
        take(2, h)
        take(6, h)
        guarded(2, h)
        r2.start(h)

    each(stage2)

    def stage5(h):
        take(3, h)
        take(5, h)
        guarded(5, h)
        r5.start(h)
        last[5].start(h)

    each(stage5)

    def stage3(h):
        guarded(3, h)
        r2.recv(h)

        @pl.when(z >= 1)
        def _():
            sbuf[1, h] = plus(dqb[1, h], rbuf[1, h])

        @pl.when(z == 0)
        def _():
            sbuf[1, h] = dqb[1, h]

        r1.start(h)

    each(stage3)

    def stage4(h):
        take(4, h)
        guarded(4, h)
        r4.start(h)

    each(stage4)

    def stage6(h):
        guarded(6, h)
        for j, slot in ((0, 1), (1, 3)):
            at = pl.ds(slot * rows, rows)
            kv1s[h, j, 0] = dkacc[h, at, :].astype(BF)
            kv1s[h, j, 1] = dvacc[h, at, :].astype(BF)
        t1.start(h)
        r4.recv(h)

        @pl.when(z >= 1)
        def _():
            sbuf[3, h] = plus(dqb[3, h], rbuf[3, h])

        @pl.when(z == 0)
        def _():
            sbuf[3, h] = dqb[3, h]

        r3.start(h)
        r5.recv(h)

        @pl.when(z <= 1)
        def _():
            sbuf[6, h] = plus(dqb[6, h], rbuf[6, h])

        r6.start(h)
        last[6].start(h)

    each(stage6)

    def fold(h):
        t1.recv(h)
        at = pl.ds(2 * rows, rows)
        kv2s[h, 0] = plus(dkacc[h, at, :], kv1r[h, 1, 0])
        kv2s[h, 1] = plus(dvacc[h, at, :], kv1r[h, 1, 1])
        t2.start(h)
        r6.recv(h)

        @pl.when(z == 0)
        def _():
            sbuf[7, h] = plus(dqb[7, h], rbuf[7, h])

        last[7].start(h)

    each(fold)

    def finish(h):
        t2.recv(h)
        at = pl.ds(0, rows)
        key_sum = dkacc[h, at, :] + kv1r[h, 0, 0].astype(F32) + kv2r[h, 0].astype(F32)
        value_sum = dvacc[h, at, :] + kv1r[h, 0, 1].astype(F32) + kv2r[h, 1].astype(F32)
        dk_out[h] = (key_sum * factor).astype(BF)
        dv_out[h] = value_sum.astype(BF)
        r1.recv(h)
        r3.recv(h)
        for r in (5, 6, 7):
            last[r].recv(h)
        for slot, cond in ((1, z >= 1), (0, z >= 3), (2, z >= 5)):
            @pl.when(cond)
            def _(slot=slot):
                dq0[h] += rown[slot, h].astype(F32)
        dq_out[h] = (dq0[h] * factor).astype(BF)

    each(finish)

    for c in channels:
        c.drain()


def body(queries, key_vectors, value_vectors, attn_output, output_grad, w_out, log_total):
    rows, heads, width = queries.shape
    major = lambda a: jnp.transpose(a, (1, 0, 2))
    block = jax.ShapeDtypeStruct((heads, rows, width), BF)
    vmem = pl.BlockSpec(memory_space=pltpu.VMEM)
    V = pltpu.VMEM
    blk = (heads, rows, width)
    outs = pl.pallas_call(
        kernel,
        out_shape=(block, block, block),
        in_specs=[vmem] * 6 + [pl.BlockSpec(memory_space=pl.ANY)],
        out_specs=(vmem, vmem, vmem),
        scratch_shapes=[
            V(w_out.shape, BF),
            V((2, Y) + output_grad.shape, BF),
            V((Z,) + blk, BF),
            V((heads, 4, rows, width), BF),
            V((heads, 4, rows, width), BF),
            V((Z,) + blk, BF),
            V((Z, 8, rows), F32),
            V((Z,) + blk, BF),
            V((Z,) + blk, BF),
            V((Z,) + blk, BF),
            V((3,) + blk, BF),
            V((heads, 4 * rows, width), F32),
            V((heads, 4 * rows, width), F32),
            V(blk, F32),
            V((heads, 2, 2, rows, width), BF),
            V((heads, 2, 2, rows, width), BF),
            V((heads, 2, rows, width), BF),
            V((heads, 2, rows, width), BF),
            pltpu.SemaphoreType.DMA,
            pltpu.SemaphoreType.DMA((COPIES,)),
            pltpu.SemaphoreType.DMA((COPIES,)),
        ],
        compiler_params=pltpu.CompilerParams(
            collective_id=0, has_side_effects=True, vmem_limit_bytes=60 * 1024 * 1024),
        name="attention_backward",
    )(
        major(queries), major(key_vectors), major(value_vectors), major(attn_output),
        output_grad, jnp.transpose(log_total, (1, 0)), w_out,
    )
    return tuple(major(a) for a in outs)


def solution(mesh):
    row = P("ctx", "head", None)
    return jax.shard_map(
        body, mesh=mesh,
        in_specs=(row, row, row, row, P("ctx", "head"), P("head", None), P("ctx", "head")),
        out_specs=(row, row, row), check_vma=False)
```

time: 94.6 us -> 91 us (0.962)
  the two profiles are of different devices: /device:TPU:1 before, /device:TPU:66 now
where the time goes in v2:
time: 91 us; the launch traced here: 90.8 us
  Pallas kernels  85.3 us (94%)
  local copies, waits for them, and re-layouts  4.85 us (5%)
    pallas_call x1, Pallas kernels, body(): pl.pallas_call(kernel, out_shape=(block, block, block), in_specs=[vmem] *...  85.3 us
    unnamed x3, local copies, waits for them, and re-layouts  4.85 us

profile of v2, /device:TPU:66, one launch (start us, length us, event | category | flops | bytes accessed | tf_op | source)
XLA Modules:
  0.0 90.8 jit_solution(11970741535630539450)
XLA Ops:
  0.6 85.3 %attention_backward.1 = (bf16[3,256,128]{2,1,0:T(8,128)(2,1)}, bf16[3,256,128]{2,1,0:T(8,128)(2,1)}, bf16[3,256,128]{2,1,0:T(8,128)(2,1)}) custom-call(bf16[3,256,128]{2,1,0:T(8,128)(2,1)} %bitcast.8, bf16[3,256,128]{2,1,0:T(8,128)(2,1)} %bitcast.9, bf16[3,256,128]{2,1,0:T(8,128)(2,1)} %bitcast.10, bf16[3,256,128]{2,1,0:T(8,128)(2,1)} %bitcast.11, ...), custom_call_target="tpu_custom_call" | custom-call | tf_op jit(solution)/shard_map/attention_backward/pallas_call | solution.py:475
  85.9 1.6 %copy.13 = bf16[256,3,128]{2,0,1:T(8,128)(2,1)} copy(bf16[256,3,128]{2,0,1:T(8,128)(2,1)} %bitcast.14) | data formatting | bytes 393216
  87.6 1.6 %copy.14 = bf16[256,3,128]{2,0,1:T(8,128)(2,1)} copy(bf16[256,3,128]{2,0,1:T(8,128)(2,1)} %bitcast.13) | data formatting | bytes 393216
  89.2 1.6 %copy.15 = bf16[256,3,128]{2,0,1:T(8,128)(2,1)} copy(bf16[256,3,128]{2,0,1:T(8,128)(2,1)} %bitcast.12) | data formatting | bytes 393216

commit v3 on v2

v3 whole, which is shorter than its diff:
```python
import math

import jax
import jax.numpy as jnp
from jax import lax
from jax.experimental import pallas as pl
from jax.experimental.pallas import tpu as pltpu
from jax.sharding import PartitionSpec as P

MESH = pl.DeviceIdType.MESH
BF = jnp.bfloat16
F32 = jnp.float32
LOG2E = math.log2(math.e)
Z = 8
Y = 4
COPIES = 320

NT = (((1,), (1,)), ((), ()))
TN = (((0,), (0,)), ((), ()))
NN = (((1,), (0,)), ((), ()))


def mm(a, b, dims):
    return lax.dot_general(a, b, dims, preferred_element_type=F32)


def plus(a, b):
    return (a.astype(F32) + b.astype(F32)).astype(BF)


def kernel(
    q_ref, k_ref, v_ref, o_ref, g_ref, lse_ref, w_hbm,
    out,
    w_vm, gall, qall, kall, vall, doall, tots, dels, probs, dqb, sbuf, rbuf, rown,
    dkacc, dvacc, dq0, kv1s, kv1r, kv2s, kv2r,
    w_sem, send_sem, recv_sem,
):
    heads, rows, width = q_ref.shape
    half = rows // 2
    factor = width ** -0.5
    ctx = lax.axis_index("ctx")
    hd = lax.axis_index("head")
    z = ctx // 4
    p = ctx % 4
    xb, cb = p // 2, p % 2
    xh, y = hd // Y, hd % Y

    def plane(to):
        return ((to + Z) % Z * 4 + p, hd)

    up, down = plane(z + 1), plane(z - 1)
    north = (ctx, xh * Y + (y + 1) % Y)
    south = (ctx, xh * Y + (y + Y - 1) % Y)
    across = (ctx, (1 - xh) * Y + y)
    side = (z * 4 + (1 - xb) * 2 + cb, hd)
    twin = (z * 4 + xb * 2 + 1 - cb, hd)
    peers = [plane(z + d) for d in (-3, -2, -1, 1, 2, 3)]
    peers += [north, south, across, side, twin]

    wcopy = pltpu.make_async_copy(w_hbm, w_vm, w_sem)
    wcopy.start()
    barrier = pltpu.get_barrier_semaphore()
    for peer in peers:
        pl.semaphore_signal(barrier, inc=1, device_id=peer, device_id_type=MESH)

    used = [0]
    channels = []

    def when(cond, act):
        if cond is None:
            act()
        else:
            pl.when(cond)(act)

    class Channel:
        def __init__(self, src, dst, to, send_if=None, recv_if=None, waves=2, m=heads, shift=0, slots=1):
            self.src, self.dst, self.to, self.shift = src, dst, to, shift
            self.send_if, self.recv_if, self.waves, self.m = send_if, recv_if, waves, m
            self.base = used[0]
            used[0] += waves * m * slots
            channels.append(self)

        def copy(self, w, h, shift):
            at = self.base + shift + w * self.m + h
            return pltpu.make_async_remote_copy(
                src_ref=self.src(w, h), dst_ref=self.dst(w, h),
                send_sem=send_sem.at[at], recv_sem=recv_sem.at[at],
                device_id=self.to, device_id_type=MESH)

        def start(self, w=0, h=0):
            when(self.send_if, lambda: self.copy(w, h, self.shift).start())

        def recv(self, w=0, h=0):
            when(self.recv_if, lambda: self.copy(w, h, 0).wait_recv())

        def recv_at(self, w, h, shift, cond):
            when(cond, lambda: self.copy(w, h, shift).wait_recv())

        def drain(self):
            def act():
                for w in range(self.waves):
                    for h in range(self.m):
                        self.copy(w, h, self.shift).wait_send()
            when(self.send_if, act)

    def once(src, dst, to, **kw):
        return Channel(lambda w, h: src, lambda w, h: dst, to, waves=1, m=1, **kw)

    def valid(r):
        return z + r <= Z - 1

    class Ring:
        def __init__(self, own, held, m):
            self.hops = {}
            self.m = m
            for r in range(1, 5):
                src = own if r == 1 else (lambda w, h, r=r: held(r - 1, w, h))
                self.hops[r] = Channel(
                    src, lambda w, h, r=r: held(r, w, h), down, m=m,
                    send_if=(z >= 1) & (z - 1 + r <= Z - 1), recv_if=valid(r))
            self.wrap = Channel(
                own, lambda w, h: held(z, w, h), plane(0), m=m, send_if=z >= 5,
                shift=(z - 5) * 2 * m, slots=3)
            self.seven = Channel(
                lambda w, h: held(7, w, h), lambda w, h: held(6, w, h), up, m=m,
                send_if=z == 0, recv_if=z == 1)
            self.six = Channel(
                lambda w, h: held(6, w, h), lambda w, h: held(5, w, h), up, m=m,
                send_if=z <= 1, recv_if=(z == 1) | (z == 2))

        def begin(self, w):
            for h in range(self.m):
                self.hops[1].start(w, h)
                self.wrap.start(w, h)

        def step(self, r, w, h):
            if r <= 4:
                self.hops[r].recv(w, h)
                if r < 4:
                    self.hops[r + 1].start(w, h)
            else:
                self.wrap.recv_at(w, h, (r - 5) * 2 * self.m, z == 0)
                if r == 7:
                    self.seven.start(w, h)
                if r == 6:
                    self.seven.recv(w, h)
                    self.six.start(w, h)
                if r == 5:
                    self.six.recv(w, h)

        def hop(self, r, w):
            for h in range(self.m):
                self.step(r, w, h)

    def cut(w, first, size):
        return pl.ds(w * half + first * half // 4, size * half // 4)

    g01 = [once(g_ref.at[cut(w, 0, 4)], gall.at[0, 1, cut(w, 0, 4)], south) for w in (0, 1)]
    g03 = [once(g_ref.at[cut(w, 0, 4)], gall.at[0, 3, cut(w, 0, 4)], north) for w in (0, 1)]
    g10 = [once(g_ref.at[cut(w, 0, 4)], gall.at[1, 0, cut(w, 0, 4)], across) for w in (0, 1)]
    g02s = [once(gall.at[0, 1, cut(w, 0, 2)], gall.at[0, 2, cut(w, 0, 2)], south) for w in (0, 1)]
    g02n = [once(gall.at[0, 3, cut(w, 2, 2)], gall.at[0, 2, cut(w, 2, 2)], north) for w in (0, 1)]
    g11 = [once(gall.at[1, 0, cut(w, 0, 4)], gall.at[1, 1, cut(w, 0, 4)], south) for w in (0, 1)]
    g13 = [once(gall.at[1, 0, cut(w, 0, 4)], gall.at[1, 3, cut(w, 0, 4)], north) for w in (0, 1)]
    g12s = [once(gall.at[1, 1, cut(w, 0, 1)], gall.at[1, 2, cut(w, 0, 1)], south) for w in (0, 1)]
    g12x = [once(gall.at[0, 2, cut(w, 1, 2)], gall.at[1, 2, cut(w, 1, 2)], across) for w in (0, 1)]
    g12n = [once(gall.at[1, 3, cut(w, 3, 1)], gall.at[1, 2, cut(w, 3, 1)], north) for w in (0, 1)]
    at_rows = lambda w: pl.ds(w * half, half)
    qring = Ring(lambda w, h: q_ref.at[h, at_rows(w)], lambda r, w, h: qall.at[r, w * heads + h], heads)
    lring = Ring(lambda w, h: tots.at[0, w], lambda r, w, h: tots.at[r, w], 1)
    k2 = once(k_ref, kall.at[:, 2], side)
    v2 = once(v_ref, vall.at[:, 2], side)
    k1 = once(k_ref, kall.at[:, 1], twin)
    v1 = once(v_ref, vall.at[:, 1], twin)
    k3 = once(kall.at[:, 2], kall.at[:, 3], twin)
    v3 = once(vall.at[:, 2], vall.at[:, 3], twin)

    dkacc[...] = jnp.zeros_like(dkacc)
    dvacc[...] = jnp.zeros_like(dvacc)
    for w in (0, 1):
        for h in range(heads):
            qall[0, w * heads + h] = q_ref[h, w * half:(w + 1) * half]
    kall[:, 0] = k_ref[...]
    vall[:, 0] = v_ref[...]
    for r in (1, 3, 5, 7):
        @pl.when(z + r >= Z)
        def _(r=r):
            qall[r] = jnp.zeros(qall.shape[1:], BF)
            doall[r] = jnp.zeros(doall.shape[1:], BF)
            tots[r] = jnp.zeros(tots.shape[1:], F32)
            dels[r] = jnp.zeros(dels.shape[1:], F32)
    for w in (0, 1):
        tots[0, w] = jnp.zeros(tots.shape[2:], F32)
        tots[0, w, 0:heads, :] = lse_ref[:, w * half:(w + 1) * half] * LOG2E
    pl.semaphore_wait(barrier, len(peers))

    sring = Ring(lambda w, h: dels.at[0, w], lambda r, w, h: dels.at[r, w], 1)
    dring = Ring(lambda w, h: doall.at[0, w * heads + h], lambda r, w, h: doall.at[r, w * heads + h], heads)

    def hop(r, w):
        sring.hop(r, w)
        dring.hop(r, w)

    def qhop(r, w):
        lring.hop(r, w)
        qring.hop(r, w)

    def proj(a, b, w):
        at = ((xh + a) % 2 * Y + (y + b) % Y) * g_ref.shape[1]
        block = g_ref[w * half:(w + 1) * half] if a == b == 0 else gall[a, b, w * half:(w + 1) * half]
        return mm(block, w_vm[:, pl.ds(pl.multiple_of(at, 128), g_ref.shape[1])], NT)

    def project(w):
        grad = acc[w].astype(BF)
        dels[0, w] = jnp.zeros(dels.shape[2:], F32)
        for h in range(heads):
            grad_h = grad[:, h * width:(h + 1) * width]
            doall[0, w * heads + h] = grad_h
            terms = grad_h.astype(F32) * o_ref[h, w * half:(w + 1) * half].astype(F32)
            delta = jnp.sum(terms, axis=1, keepdims=True)
            dels[0, w, h:h + 1, :] = jnp.transpose(
                jnp.broadcast_to(delta, (half, 128)), (1, 0))[0:1, :]
        sring.begin(w)
        dring.begin(w)

    def line(ref, a, w, h):
        return jnp.concatenate([ref[a, w, pl.ds(h, 1), :], ref[a + 1, w, pl.ds(h, 1), :]], axis=1)

    def both(ref, a, w, h):
        i = w * heads + h
        return jnp.concatenate([ref[a, i], ref[a + 1, i]], axis=0)

    def prob_of(a, w, h):
        keys = kall[h].reshape(4 * rows, width)
        raw = mm(keys, both(qall, a, w, h), NT)
        shifted = raw * (factor * LOG2E) - line(tots, a, w, h)
        if a == 0:
            row = lax.broadcasted_iota(jnp.int32, shifted.shape, 0)
            col = lax.broadcasted_iota(jnp.int32, shifted.shape, 1)
            offs = []
            for j in range(4):
                jx, jc = j // 2, j % 2
                pj = (xb + jx) % 2 * 2 + (cb + jc) % 2
                offs.append((pj - p - j) * rows)
            off = jnp.where(
                row < 2 * rows,
                jnp.where(row < rows, offs[0], offs[1]),
                jnp.where(row < 3 * rows, offs[2], offs[3]))
            shown = (row + off <= col + w * half) | (col >= half)
            shifted = jnp.where(shown, shifted, -jnp.inf)
        return jnp.exp2(shifted)

    def front(a, w, h):
        probs[a + w, h] = prob_of(a, w, h)

    def tile(a, w, h):
        i = w * heads + h
        keys = kall[h].reshape(4 * rows, width)
        values = vall[h].reshape(4 * rows, width)
        query = both(qall, a, w, h)
        grad = both(doall, a, w, h)
        prob = probs[a + w, h] if a <= 2 else prob_of(a, w, h)
        pgrad = mm(values, grad, NT)
        score = (prob * (pgrad - line(dels, a, w, h))).astype(BF)
        dvacc[h] += mm(prob.astype(BF), grad, NN)
        dkacc[h] += mm(score, query, NN)
        part = mm(score, keys, TN)
        if a == 0:
            dq0[i] = part[:half]
        else:
            dqb[a, i] = part[:half].astype(BF)
        dqb[a + 1, i] = part[half:].astype(BF)

    def each(act):
        def one(h, carry):
            act(h)
            return carry
        lax.fori_loop(0, heads, one, 0)

    def serve(hops, h):
        if hops:
            @pl.when(h == 0)
            def _():
                for r, w in hops:
                    sring.hop(r, w)
            for r, w in hops:
                dring.step(r, w, h)

    def fronts(a, w, hops=()):
        def act(h):
            serve(hops, h)
            if a == 0:
                front(a, w, h)
            else:
                pl.when(valid(a))(lambda: front(a, w, h))
        each(act)

    def tiles(a, w, hops=(), then=None):
        def act(h):
            serve(hops, h)
            if a == 0:
                tile(a, w, h)
            else:
                pl.when(valid(a))(lambda: tile(a, w, h))
            if then is not None:
                then(h)
        each(act)

    def of(ref, r):
        return lambda w, h: ref.at[r, w * heads + h]

    r2 = Channel(of(dqb, 2), of(rbuf, 1), up, send_if=valid(2), recv_if=(z >= 1) & valid(1))
    r1 = Channel(of(sbuf, 1), of(rown, 1), up, send_if=valid(1), recv_if=z >= 1)
    r4 = Channel(of(dqb, 4), of(rbuf, 3), up, send_if=valid(4), recv_if=(z >= 1) & valid(3))
    r3 = Channel(of(sbuf, 3), of(rown, 0), plane(z + 3), send_if=valid(3), recv_if=z >= 3)
    wrapped = {
        r: Channel(
            of(dqb, r), lambda w, h: rown.at[2 + z % 5, w * heads + h], plane(z + r),
            send_if=valid(r), recv_if=z >= r)
        for r in (5, 6, 7)
    }
    t1 = Channel(lambda w, h: kv1s.at[h], lambda w, h: kv1r.at[h], twin, waves=1)
    t2 = Channel(lambda w, h: kv2s.at[h], lambda w, h: kv2r.at[h], side, waves=1)

    def merge(r, w, h, got, alone):
        i = w * heads + h

        @pl.when(got)
        def _():
            sbuf[r, i] = plus(dqb[r, i], rbuf[r, i])

        if alone is not None:
            @pl.when(alone)
            def _():
                sbuf[r, i] = dqb[r, i]

    def near(w):
        def act(h):
            r2.recv(w, h)
            merge(1, w, h, z >= 1, z == 0)
            r1.start(w, h)
        each(act)

    def far(w):
        def act(h):
            r4.recv(w, h)
            merge(3, w, h, z >= 1, z == 0)
            r3.start(w, h)
        each(act)

    def send2(w):
        return lambda h: r2.start(w, h)

    def send45(w):
        def then(h):
            r4.start(w, h)
            wrapped[5].start(w, h)
        return then

    def send67(w):
        def then(h):
            wrapped[6].start(w, h)
            wrapped[7].start(w, h)
        return then

    def hand_over(h):
        send67(1)(h)
        for j, slot in ((0, 1), (1, 3)):
            at = pl.ds(slot * rows, rows)
            kv1s[h, j, 0] = dkacc[h, at, :].astype(BF)
            kv1s[h, j, 1] = dvacc[h, at, :].astype(BF)
        t1.start(0, h)

    def fold(h):
        t1.recv(0, h)
        at = pl.ds(2 * rows, rows)
        kv2s[h, 0] = plus(dkacc[h, at, :], kv1r[h, 1, 0])
        kv2s[h, 1] = plus(dvacc[h, at, :], kv1r[h, 1, 1])
        t2.start(0, h)

    g01[0].start()
    g03[0].start()
    g10[0].start()
    lring.begin(0)
    qring.begin(0)
    g01[1].start()
    g03[1].start()
    g10[1].start()
    lring.begin(1)
    qring.begin(1)
    k2.start()
    k1.start()
    v2.start()
    v1.start()
    wcopy.wait()

    acc = [proj(0, 0, 0), proj(0, 0, 1)]
    qhop(1, 0)
    g01[0].recv()
    g02s[0].start()
    g03[0].recv()
    g02n[0].start()
    g10[0].recv()
    g11[0].start()
    g13[0].start()
    qhop(1, 1)
    acc[0] += proj(0, 1, 0)
    acc[0] += proj(0, 3, 0)
    acc[0] += proj(1, 0, 0)
    g01[1].recv()
    g02s[1].start()
    g03[1].recv()
    g02n[1].start()
    qhop(2, 0)
    g02s[0].recv()
    g02n[0].recv()
    g12x[0].start()
    qhop(2, 1)
    k1.recv()
    k2.recv()
    k3.start()
    acc[0] += proj(0, 2, 0)
    acc[1] += proj(0, 1, 1)
    acc[1] += proj(0, 3, 1)
    qhop(3, 0)
    g11[0].recv()
    g12s[0].start()
    g13[0].recv()
    g12n[0].start()
    g10[1].recv()
    g11[1].start()
    g13[1].start()
    acc[0] += proj(1, 1, 0)
    acc[0] += proj(1, 3, 0)
    acc[1] += proj(1, 0, 1)
    k3.recv()
    fronts(0, 0)
    qhop(3, 1)
    g02s[1].recv()
    g02n[1].recv()
    g12x[1].start()
    for c in (g12s[0], g12n[0], g12x[0]):
        c.recv()
    acc[0] += proj(1, 2, 0)
    project(0)
    v2.recv()
    v3.start()
    g11[1].recv()
    g12s[1].start()
    g13[1].recv()
    g12n[1].start()
    qhop(7, 0)
    qhop(7, 1)
    fronts(0, 1)
    acc[1] += proj(0, 2, 1)
    acc[1] += proj(1, 1, 1)
    acc[1] += proj(1, 3, 1)
    hop(1, 0)
    for c in (g12s[1], g12n[1], g12x[1]):
        c.recv()
    acc[1] += proj(1, 2, 1)
    project(1)
    v1.recv()
    v3.recv()
    fronts(2, 0, [(2, 0)])
    qhop(6, 0)
    qhop(6, 1)
    qhop(4, 0)
    tiles(0, 0, [(1, 1)])
    fronts(2, 1, [(3, 0)])
    tiles(2, 0, [(7, 0), (2, 1)], send2(0))
    qhop(5, 0)
    qhop(4, 1)
    tiles(0, 1, [(4, 0), (6, 0)])
    qhop(5, 1)
    tiles(4, 0, [(3, 1), (5, 0)], send45(0))
    tiles(2, 1, [(7, 1)], send2(1))
    near(0)
    tiles(6, 0, [(4, 1), (6, 1)], send67(0))
    far(0)

    def final(h):
        serve([(5, 1)], h)
        pl.when(valid(4))(lambda: tile(4, 1, h))
        send45(1)(h)
        pl.when(valid(6))(lambda: tile(6, 1, h))
        hand_over(h)

        @pl.when(h > 0)
        def _():
            fold(h - 1)

    each(final)
    fold(heads - 1)
    near(1)
    far(1)

    def finish(h):
        for w in (0, 1):
            i = w * heads + h
            r1.recv(w, h)
            r3.recv(w, h)
            for r in (5, 6, 7):
                wrapped[r].recv(w, h)
            for slot, cond in ((1, z >= 1), (0, z >= 3)) + tuple((2 + z - r, z >= r) for r in (5, 6, 7)):
                @pl.when(cond)
                def _(slot=slot, i=i):
                    dq0[i] += rown[slot, i].astype(F32)
            out[0, h, at_rows(w)] = (dq0[i] * factor).astype(BF)
        t2.recv(0, h)
        at = pl.ds(0, rows)
        key_sum = dkacc[h, at, :] + kv1r[h, 0, 0].astype(F32) + kv2r[h, 0].astype(F32)
        value_sum = dvacc[h, at, :] + kv1r[h, 0, 1].astype(F32) + kv2r[h, 1].astype(F32)
        out[1, h] = (key_sum * factor).astype(BF)
        out[2, h] = value_sum.astype(BF)

    each(finish)

    for c in channels:
        c.drain()


def body(queries, key_vectors, value_vectors, attn_output, output_grad, w_out, log_total):
    rows, heads, width = queries.shape
    major = lambda a: jnp.transpose(a, (1, 0, 2))
    vmem = pl.BlockSpec(memory_space=pltpu.VMEM)
    V = pltpu.VMEM
    blk = (heads, rows, width)
    chunks = (2 * heads, rows // 2, width)
    outs = pl.pallas_call(
        kernel,
        out_shape=jax.ShapeDtypeStruct((3,) + blk, BF),
        in_specs=[vmem] * 6 + [pl.BlockSpec(memory_space=pl.ANY)],
        out_specs=vmem,
        scratch_shapes=[
            V(w_out.shape, BF),
            V((2, Y) + output_grad.shape, BF),
            V((Z,) + chunks, BF),
            V((heads, 4, rows, width), BF),
            V((heads, 4, rows, width), BF),
            V((Z,) + chunks, BF),
            V((Z, 2, 8, rows // 2), F32),
            V((Z, 2, 8, rows // 2), F32),
            V((4, heads, 4 * rows, rows), F32),
            V((Z,) + chunks, BF),
            V((Z,) + chunks, BF),
            V((Z,) + chunks, BF),
            V((5,) + chunks, BF),
            V((heads, 4 * rows, width), F32),
            V((heads, 4 * rows, width), F32),
            V(chunks, F32),
            V((heads, 2, 2, rows, width), BF),
            V((heads, 2, 2, rows, width), BF),
            V((heads, 2, rows, width), BF),
            V((heads, 2, rows, width), BF),
            pltpu.SemaphoreType.DMA,
            pltpu.SemaphoreType.DMA((COPIES,)),
            pltpu.SemaphoreType.DMA((COPIES,)),
        ],
        compiler_params=pltpu.CompilerParams(
            collective_id=0, has_side_effects=True, vmem_limit_bytes=60 * 1024 * 1024),
        name="attention_backward",
    )(
        major(queries), major(key_vectors), major(value_vectors), major(attn_output),
        output_grad, jnp.transpose(log_total, (1, 0)), w_out,
    )
    return tuple(major(outs[i]) for i in range(3))


def solution(mesh):
    row = P("ctx", "head", None)
    return jax.shard_map(
        body, mesh=mesh,
        in_specs=(row, row, row, row, P("ctx", "head"), P("head", None), P("ctx", "head")),
        out_specs=(row, row, row), check_vma=False)
```

time: 91 us -> 82.9 us (0.911)
  the two profiles are of different devices: /device:TPU:66 before, /device:TPU:1 now
where the time goes in v3:
time: 82.9 us; the launch traced here: 81.7 us
  Pallas kernels  79.2 us (96%)
  local copies, waits for them, and re-layouts  1.94 us (2%)
    pallas_call x1, Pallas kernels, body(): pl.pallas_call(kernel, out_shape=jax.ShapeDtypeStruct((3,) + blk, BF), in...  79.2 us
    transpose x1, local copies, waits for them, and re-layouts, body(): major = lambda a: jnp.transpose(a, (1, 0, 2))  1.94 us

profile of v3, /device:TPU:1, one launch (start us, length us, event | category | flops | bytes accessed | tf_op | source)
XLA Modules:
  0.0 81.7 jit_solution(6751556066356832816)
XLA Ops:
  0.6 79.2 %attention_backward.1 = bf16[3,3,256,128]{3,2,1,0:T(8,128)(2,1)} custom-call(bf16[3,256,128]{2,1,0:T(8,128)(2,1)} %bitcast.17, bf16[3,256,128]{2,1,0:T(8,128)(2,1)} %bitcast.18, bf16[3,256,128]{2,1,0:T(8,128)(2,1)} %bitcast.19, bf16[3,256,128]{2,1,0:T(8,128)(2,1)} %bitcast.20, bf16[256,640]{1,0:T(8,128)(2,1)} %g_ref.1, f32[3,256]{1,0:T(4,128)} %bitcast.21, ...), custom_call_target="tpu_custom_call" | custom-call | tf_op jit(solution)/shard_map/attention_backward/pallas_call | solution.py:530
  79.8 1.9 %slice_bitcast_fusion = (bf16[256,3,128]{2,0,1:T(8,128)(2,1)}, bf16[256,3,128]{2,0,1:T(8,128)(2,1)}, bf16[256,3,128]{2,0,1:T(8,128)(2,1)}) fusion(bf16[3,3,256,128]{3,2,1,0:T(8,128)(2,1)} %attention_backward.1), kind=kLoop, calls=%fused_computation | loop fusion | bytes 1179648 | tf_op jit(solution)/shard_map/transpose | solution.py:525

commit v4 on v3

--- a/solution.py
+++ b/solution.py
@@ -334,19 +334,15 @@
             def _():
                 sbuf[r, i] = dqb[r, i]
 
-    def near(w):
-        def act(h):
-            r2.recv(w, h)
-            merge(1, w, h, z >= 1, z == 0)
-            r1.start(w, h)
-        each(act)
-
-    def far(w):
-        def act(h):
-            r4.recv(w, h)
-            merge(3, w, h, z >= 1, z == 0)
-            r3.start(w, h)
-        each(act)
+    def near(w, h):
+        r2.recv(w, h)
+        merge(1, w, h, z >= 1, z == 0)
+        r1.start(w, h)
+
+    def far(w, h):
+        r4.recv(w, h)
+        merge(3, w, h, z >= 1, z == 0)
+        r3.start(w, h)
 
     def send2(w):
         return lambda h: r2.start(w, h)
@@ -364,7 +360,6 @@
         return then
 
     def hand_over(h):
-        send67(1)(h)
         for j, slot in ((0, 1), (1, 3)):
             at = pl.ds(slot * rows, rows)
             kv1s[h, j, 0] = dkacc[h, at, :].astype(BF)
@@ -471,29 +466,33 @@
     tiles(2, 0, [(7, 0), (2, 1)], send2(0))
     qhop(5, 0)
     qhop(4, 1)
-    tiles(0, 1, [(4, 0), (6, 0)])
+    tiles(0, 1, [(4, 0), (6, 0), (7, 1)])
     qhop(5, 1)
-    tiles(4, 0, [(3, 1), (5, 0)], send45(0))
-    tiles(2, 1, [(7, 1)], send2(1))
-    near(0)
-    tiles(6, 0, [(4, 1), (6, 1)], send67(0))
-    far(0)
-
-    def final(h):
-        serve([(5, 1)], h)
-        pl.when(valid(4))(lambda: tile(4, 1, h))
-        send45(1)(h)
+    tiles(4, 0, [(3, 1), (5, 0), (6, 1)], send45(0))
+    each(lambda h: near(0, h))
+
+    def rest(h):
+        pl.when(valid(2))(lambda: tile(2, 1, h))
+        send2(1)(h)
+        pl.when(valid(6))(lambda: tile(6, 0, h))
+        send67(0)(h)
         pl.when(valid(6))(lambda: tile(6, 1, h))
-        hand_over(h)
+        send67(1)(h)
 
         @pl.when(h > 0)
         def _():
             fold(h - 1)
 
-    each(final)
+        serve([(4, 1), (5, 1)], h)
+        pl.when(valid(4))(lambda: tile(4, 1, h))
+        send45(1)(h)
+        hand_over(h)
+        far(0, h)
+
+    each(rest)
     fold(heads - 1)
-    near(1)
-    far(1)
+    each(lambda h: near(1, h))
+    each(lambda h: far(1, h))
 
     def finish(h):
         for w in (0, 1):

time: 82.9 us -> 81.9 us (0.988)
  no operation moved by 1% of the time
where the time goes in v4:
time: 81.9 us; the launch traced here: 81.1 us
  Pallas kernels  78.6 us (96%)
  local copies, waits for them, and re-layouts  1.94 us (2%)
    pallas_call x1, Pallas kernels, body(): pl.pallas_call(kernel, out_shape=jax.ShapeDtypeStruct((3,) + blk, BF), in...  78.6 us
    transpose x1, local copies, waits for them, and re-layouts, body(): major = lambda a: jnp.transpose(a, (1, 0, 2))  1.94 us

profile of v4, /device:TPU:1, one launch (start us, length us, event | category | flops | bytes accessed | tf_op | source)
XLA Modules:
  0.0 81.1 jit_solution(3425471938590523224)
XLA Ops:
  0.6 78.6 %attention_backward.1 = bf16[3,3,256,128]{3,2,1,0:T(8,128)(2,1)} custom-call(bf16[3,256,128]{2,1,0:T(8,128)(2,1)} %bitcast.17, bf16[3,256,128]{2,1,0:T(8,128)(2,1)} %bitcast.18, bf16[3,256,128]{2,1,0:T(8,128)(2,1)} %bitcast.19, bf16[3,256,128]{2,1,0:T(8,128)(2,1)} %bitcast.20, bf16[256,640]{1,0:T(8,128)(2,1)} %g_ref.1, f32[3,256]{1,0:T(4,128)} %bitcast.21, ...), custom_call_target="tpu_custom_call" | custom-call | tf_op jit(solution)/shard_map/attention_backward/pallas_call | solution.py:529
  79.2 1.9 %slice_bitcast_fusion = (bf16[256,3,128]{2,0,1:T(8,128)(2,1)}, bf16[256,3,128]{2,0,1:T(8,128)(2,1)}, bf16[256,3,128]{2,0,1:T(8,128)(2,1)}) fusion(bf16[3,3,256,128]{3,2,1,0:T(8,128)(2,1)} %attention_backward.1), kind=kLoop, calls=%fused_computation | loop fusion | bytes 1179648 | tf_op jit(solution)/shard_map/transpose | solution.py:524

commit v5 on v4

--- a/solution.py
+++ b/solution.py
@@ -491,8 +491,12 @@
 
     each(rest)
     fold(heads - 1)
-    each(lambda h: near(1, h))
-    each(lambda h: far(1, h))
+
+    def returns(h):
+        near(1, h)
+        far(1, h)
+
+    each(returns)
 
     def finish(h):
         for w in (0, 1):

time: 81.9 us -> 81.9 us (level)
  no operation moved by 1% of the time
where the time goes in v5:
time: 81.9 us; the launch traced here: 81.1 us
  Pallas kernels  78.6 us (96%)
  local copies, waits for them, and re-layouts  1.94 us (2%)
    pallas_call x1, Pallas kernels, body(): pl.pallas_call(kernel, out_shape=jax.ShapeDtypeStruct((3,) + blk, BF), in...  78.6 us
    transpose x1, local copies, waits for them, and re-layouts, body(): major = lambda a: jnp.transpose(a, (1, 0, 2))  1.94 us

profile of v5, /device:TPU:1, one launch (start us, length us, event | category | flops | bytes accessed | tf_op | source)
XLA Modules:
  0.0 81.1 jit_solution(6720358732446825670)
XLA Ops:
  0.6 78.6 %attention_backward.1 = bf16[3,3,256,128]{3,2,1,0:T(8,128)(2,1)} custom-call(bf16[3,256,128]{2,1,0:T(8,128)(2,1)} %bitcast.17, bf16[3,256,128]{2,1,0:T(8,128)(2,1)} %bitcast.18, bf16[3,256,128]{2,1,0:T(8,128)(2,1)} %bitcast.19, bf16[3,256,128]{2,1,0:T(8,128)(2,1)} %bitcast.20, bf16[256,640]{1,0:T(8,128)(2,1)} %g_ref.1, f32[3,256]{1,0:T(4,128)} %bitcast.21, ...), custom_call_target="tpu_custom_call" | custom-call | tf_op jit(solution)/shard_map/attention_backward/pallas_call | solution.py:533
  79.2 1.9 %slice_bitcast_fusion = (bf16[256,3,128]{2,0,1:T(8,128)(2,1)}, bf16[256,3,128]{2,0,1:T(8,128)(2,1)}, bf16[256,3,128]{2,0,1:T(8,128)(2,1)}) fusion(bf16[3,3,256,128]{3,2,1,0:T(8,128)(2,1)} %attention_backward.1), kind=kLoop, calls=%fused_computation | loop fusion | bytes 1179648 | tf_op jit(solution)/shard_map/transpose | solution.py:528
